TPU v7x, 512 devices: a whole 4x8x8 slice. The times are simulated.
512 devices in a mesh: leaf: 32 (over x, y), front: 16 (over z, core).
Axes of the slice: x: 4, y: 8, z: 8, core: 2. Of those that a mesh axis runs over, the one named last changes fastest.
Arguments:
- child_pivot: float32 [32, 512, 512], P('leaf', 'front')
- child_panel: float32 [32, 2048, 512], P('leaf', 'front'), may hold values from -0.9 to 0.9
- anc_front: float32 [32, 16, 512, 512], P('leaf', 'front')
- dest_list: int32 [32, 16], replicated, may hold values from 0 to 31, as said below
- col_list: int32 [32, 16], replicated, may hold values from 0 to 3, as said below
- row_list: int32 [32, 16], replicated, may hold values from 0 to 3, as said below
Outputs:
- child_lower: float32 [32, 512, 512], P('leaf', 'front')
- child_factor: float32 [32, 2048, 512], P('leaf', 'front')
- anc_factor: float32 [32, 16, 512, 512], P('leaf', 'front')
Inputs may be any that keep to these rules, and one draw needn't show every extreme that they name: dest_list[g, j] is g with exactly one bit of its index flipped; every group that row g names is named there by exactly 4 column blocks, so row g names 4 different groups. `col_list`: column blocks of one group that name the same group in dest_list have different entries here. row_list[g, f] is 1 or more for f < 4.
All inputs are finite; a program needn't handle non-finite values.
Results may differ from a plain program's by a relative error of at most 0.0001.
Values sent between devices are 32-bit elements; how exact they have to be, the bound alone decides.
No kernel may reach another device: no remote copies, remote signals or barrier semaphores. Data moves between devices by JAX's collectives and lax.ppermute only.
A program may use at most 64 MiB of HBM per device.

v0:
```python
import jax
import jax.numpy as jnp
from jax import lax
from jax.sharding import PartitionSpec as P


def swapped(value, axis, distance):
    mask = 2**distance
    pairs = [(source, source ^ mask) for source in range(lax.axis_size(axis))]
    return lax.ppermute(value, axis, pairs)


def schur_block(left, right):
    return lax.dot_general(
        left,
        right,
        (((1,), (1,)), ((), ())),
        precision=lax.Precision.HIGHEST,
        preferred_element_type=jnp.float32,
    )


def slot_ranks(dest_list):
    count = dest_list.shape[1]
    positions = jnp.arange(count, dtype=jnp.int32)
    earlier = positions[:, None] > positions[None, :]
    same = dest_list[:, :, None] == dest_list[:, None, :]
    return jnp.sum((same & earlier[None]).astype(jnp.int32), axis=2)


def lookup_rows(table, sender_ids):
    leaf_ids = jnp.arange(table.shape[0], dtype=jnp.int32)
    hits = (sender_ids[:, None] == leaf_ids[None, :]).astype(jnp.int32)
    return jnp.sum(hits[:, :, None] * table[None], axis=1)


def pick_blocks(own_targets, own_ranks, target, slot_ids, update_blocks):
    select = ((own_targets[None, :] == target) & (own_ranks[None, :] == slot_ids[:, None])).astype(
        jnp.float32
    )
    return jnp.einsum("kj,xjy->kxy", select, update_blocks, precision=lax.Precision.HIGHEST)


def per_device(child_pivot, child_panel, anc_front, dest_list, col_list, row_list):
    front_count = lax.axis_size("front")
    front_pos = lax.axis_index("front")
    group = lax.axis_index("leaf")
    slab = child_pivot.shape[1]
    block = child_panel.shape[1]
    width = child_panel.shape[2]
    blocks_wide = width // block
    row_slots = anc_front.shape[2] // block
    pivot = lax.all_gather(child_pivot[0], "front", axis=0, tiled=True)
    lower = jnp.linalg.cholesky(pivot)
    lower_rows = lax.dynamic_slice_in_dim(lower, front_pos * slab, slab, 0)
    panel = lax.linalg.triangular_solve(
        lower, child_panel[0], left_side=False, lower=True, transpose_a=True
    )
    update = schur_block(panel, lax.all_gather(panel, "front", axis=0, tiled=True))
    ranks = slot_ranks(dest_list)
    slot_ids = jnp.arange(blocks_wide, dtype=jnp.int32)
    own_targets = lax.dynamic_index_in_dim(dest_list, group, 0, keepdims=False)
    own_ranks = lax.dynamic_index_in_dim(ranks, group, 0, keepdims=False)
    update_blocks = update.reshape(block, front_count, block)
    levels = lax.axis_size("leaf").bit_length() - 1
    arrived = []
    partners = []
    for level_bit in range(levels):
        partner = jnp.bitwise_xor(group, 1 << level_bit)
        outgoing = pick_blocks(own_targets, own_ranks, partner, slot_ids, update_blocks)
        arrived.append(swapped(outgoing, "leaf", level_bit))
        partners.append(partner)
    received = jnp.stack(arrived)
    sender_ids = jnp.stack(partners)
    src_dest = lookup_rows(dest_list, sender_ids)
    src_ranks = lookup_rows(ranks, sender_ids)
    src_cols = lookup_rows(col_list, sender_ids)
    src_rows = lookup_rows(row_list, sender_ids)
    match = (src_dest == group)[:, None, :] & (src_ranks[:, None, :] == slot_ids[None, :, None])
    live = jnp.sum(match.astype(jnp.int32), axis=2)
    column_of = jnp.sum(jnp.where(match, src_cols[:, None, :], 0), axis=2)
    row_of = lax.dynamic_index_in_dim(src_rows, front_pos, 1, keepdims=False)
    slot_rows = jnp.arange(row_slots, dtype=jnp.int32)
    slot_cols = jnp.arange(blocks_wide, dtype=jnp.int32)
    weight = (
        (live[:, :, None, None] == 1)
        & (row_of[:, None, None, None] == slot_rows[None, None, :, None])
        & (column_of[:, :, None, None] == slot_cols[None, None, None, :])
    ).astype(jnp.float32)
    incoming = jnp.einsum("gkrc,gkxy->rxcy", weight, received, precision=lax.Precision.HIGHEST)
    assembled = anc_front[0, 0] - incoming.reshape(row_slots * block, width)
    owner = front_pos < blocks_wide
    owner_pos = jnp.minimum(front_pos, blocks_wide - 1)
    top_rows = jnp.where(owner, assembled[:block], 0.0)
    contribution = lax.dynamic_update_slice_in_dim(
        jnp.zeros((width, width), jnp.float32), top_rows, owner_pos * block, 0
    )
    anc_pivot = lax.psum(contribution, "front")
    anc_lower = jnp.linalg.cholesky(anc_pivot)
    solved = lax.linalg.triangular_solve(
        anc_lower, assembled, left_side=False, lower=True, transpose_a=True
    )
    own_lower = lax.dynamic_slice_in_dim(anc_lower, owner_pos * block, block, 0)
    padded = lax.dynamic_update_slice_in_dim(jnp.zeros_like(solved), own_lower, 0, 0)
    row_ids = jnp.arange(row_slots * block, dtype=jnp.int32)
    mask = (row_ids < block)[:, None] & owner
    anc_out = jnp.where(mask, padded, solved)
    return (lower_rows[None], panel[None], anc_out[None, None])


def solution(mesh):
    in_specs = (
        P("leaf", "front", None),
        P("leaf", "front", None),
        P("leaf", "front", None, None),
        P(),
        P(),
        P(),
    )
    out_specs = (P("leaf", "front", None), P("leaf", "front", None), P("leaf", "front", None, None))
    return jax.shard_map(
        per_device, mesh=mesh, in_specs=in_specs, out_specs=out_specs, check_vma=False
    )
```

profile of v0, /device:TPU:1, one launch (start us, length us, event | category | flops | bytes accessed | tf_op | source)
XLA Modules:
  0.0 557.9 jit_solution(7262948002128751580)
XLA Ops:
  7.2 1.5 copy.131
  8.8 49.6 %all-gather.6.cloned.1.call-done = f32[1,512,512]{2,0,1:T(1,128)} async-done(((f32[1,32,512]{2,0,1:T(1,128)}), f32[1,512,512]{2,0,1:T(1,128)}) %all-gather.6.cloned.1.call-update) | async-done | bytes 1048592 | tf_op jit(solution)/shard_map/all_gather | solution.py:53
  58.5 2.4 copy.132
  61.2 11.7 %cholesky.286 = f32[128,128]{1,0:T(8,128)S(1)} custom-call(f32[128,128]{1,0:T(8,128)S(1)} %cholesky.426), custom_call_target="Cholesky" | custom-call | tf_op jit(solution)/shard_map/jit(cholesky)/cholesky | solution.py:54
  73.0 9.8 %custom-call.31 = f32[1,128,128]{1,2,0:T(8,128)S(1)} custom-call(f32[1,128,128]{2,1,0:T(8,128)S(1)} %get-tuple-element.123), custom_call_target="InvertDiagBlocksLowerTriangular" | custom-call | tf_op jit(solution)/shard_map/jit(cholesky)/cholesky | solution.py:54
  83.6 11.7 %cholesky.305 = f32[128,128]{1,0:T(8,128)S(1)} custom-call(f32[128,128]{1,0:T(8,128)S(1)} %cholesky.430), custom_call_target="Cholesky" | custom-call | tf_op jit(solution)/shard_map/jit(cholesky)/cholesky | solution.py:54
  95.5 10.0 %custom-call.32 = f32[1,128,128]{1,2,0:T(8,128)S(1)} custom-call(f32[1,128,128]{2,1,0:T(8,128)S(1)} %get-tuple-element.121), custom_call_target="InvertDiagBlocksLowerTriangular" | custom-call | tf_op jit(solution)/shard_map/jit(cholesky)/cholesky | solution.py:54
  106.6 11.7 %cholesky.326 = f32[128,128]{1,0:T(8,128)S(1)} custom-call(f32[128,128]{1,0:T(8,128)S(1)} %cholesky.435), custom_call_target="Cholesky" | custom-call | tf_op jit(solution)/shard_map/jit(cholesky)/cholesky | solution.py:54
  118.4 9.8 %custom-call.33 = f32[1,128,128]{1,2,0:T(8,128)S(1)} custom-call(f32[1,128,128]{2,1,0:T(8,128)S(1)} %get-tuple-element.119), custom_call_target="InvertDiagBlocksLowerTriangular" | custom-call | tf_op jit(solution)/shard_map/jit(cholesky)/cholesky | solution.py:54
  129.1 12.1 %cholesky.343 = f32[128,128]{1,0:T(8,128)S(1)} custom-call(f32[128,128]{1,0:T(8,128)S(1)} %convolution_subtract_fusion.11), custom_call_target="Cholesky" | custom-call | tf_op jit(solution)/shard_map/jit(cholesky)/cholesky | solution.py:54
  141.3 0.6 compare_reduce_fusion.10
  141.9 0.7 compare_reduce_fusion.9
  142.6 0.6 compare_reduce_fusion.11
  145.9 1.2 fusion.5
  147.2 8.5 %while.2 = (s32[]{:T(128)}, f32[512,512]{0,1:T(8,128)S(1)}, s32[4,2]{0,1:T(2,128)S(1)}, f32[4,128,128]{2,1,0:T(8,128)S(1)}, s32[]{:T(128)}) while((s32[]{:T(128)}, f32[512,512]{0,1:T(8,128)S(1)}, s32[4,2]{0,1:T(2,128)S(1)}, f32[4,128,128]{2,1,0:T(8,128)S(1)}, s32[]{:T(128)}) %tuple.71), condition=%wide.while_cond, body=%wide.while_body.sunk | while | flops 2 | bytes 393329 | solution.py:56
  147.8 1.4 dynamic-slice.13
  149.9 1.4 dynamic-slice.13
  152.0 1.4 dynamic-slice.13
  154.1 1.4 dynamic-slice.13
  155.6 39.3 %custom-call.26 = f32[4,128,128]{1,2,0:T(8,128)S(1)} custom-call(f32[4,128,128]{2,1,0:T(8,128)S(1)} %get-tuple-element.11), custom_call_target="InvertDiagBlocksLowerTriangular" | custom-call | tf_op jit(solution)/shard_map/triangular_solve | solution.py:56
  197.3 0.7 pad_maximum_fusion
  198.2 1.6 copy.143
  201.5 47.6 %all-gather.4.cloned.1.call-done = f32[2048,512]{0,1:T(8,128)} async-done(((f32[128,512]{0,1:T(8,128)}), f32[2048,512]{0,1:T(8,128)}) %all-gather.4.cloned.1.call-update) | async-done | bytes 4194320 | tf_op jit(solution)/shard_map/all_gather | solution.py:59
  249.1 4.5 convolution_bitcast_fusion
  254.3 2.6 collective-permute-start
  257.3 4.0 collective-permute-start.1
  261.9 4.4 collective-permute-start.2
  266.7 3.1 collective-permute-start.3
  270.3 4.5 collective-permute-start.4
  274.9 9.5 %collective-permute-done.1 = f32[4,128,128]{2,0,1:T(4,128)S(1)} collective-permute-done((f32[4,128,128]{2,0,1:T(4,128)S(1)}, f32[4,128,128]{2,0,1:T(4,128)S(1)}, u32[]{:S(2)}, u32[]{:S(2)}) %collective-permute-start.1) | collective-permute-done | bytes 262176 | tf_op jit(solution)/shard_map/ppermute | solution.py:10
  284.6 1.2 convolution_bitcast_fusion.1
  286.7 1.0 copy-done.2
  287.8 1.1 constant_dynamic-slice_fusion.3
  288.9 0.7 copy.141
  289.6 0.8 copy.158
  290.5 113.9 %all-reduce.4.cloned.1.call-done = f32[512,512]{0,1:T(8,128)} async-done(((f32[512,512]{0,1:T(8,128)}), f32[512,512]{0,1:T(8,128)}) %all-reduce.4.cloned.1.call-update) | async-done | bytes 1048592 | tf_op jit(solution)/shard_map/psum | solution.py:98
  404.4 1.6 copy.146
  406.3 1.0 copy-done.3
  407.3 11.7 %cholesky.358 = f32[128,128]{1,0:T(8,128)S(1)} custom-call(f32[128,128]{1,0:T(8,128)S(1)} %cholesky.439), custom_call_target="Cholesky" | custom-call | tf_op jit(solution)/shard_map/jit(cholesky)/cholesky | solution.py:99
  419.1 9.8 %custom-call.34 = f32[1,128,128]{1,2,0:T(8,128)S(1)} custom-call(f32[1,128,128]{2,1,0:T(8,128)S(1)} %get-tuple-element.117), custom_call_target="InvertDiagBlocksLowerTriangular" | custom-call | tf_op jit(solution)/shard_map/jit(cholesky)/cholesky | solution.py:99
  428.9 1.2 fusion.21
  430.3 1.3 convolution_subtract_fusion.3
  431.6 11.9 %cholesky.377 = f32[128,128]{1,0:T(8,128)S(1)} custom-call(f32[128,128]{1,0:T(8,128)S(1)} %cholesky.443), custom_call_target="Cholesky" | custom-call | tf_op jit(solution)/shard_map/jit(cholesky)/cholesky | solution.py:99
  443.6 9.8 %custom-call.35 = f32[1,128,128]{1,2,0:T(8,128)S(1)} custom-call(f32[1,128,128]{2,1,0:T(8,128)S(1)} %get-tuple-element.115), custom_call_target="InvertDiagBlocksLowerTriangular" | custom-call | tf_op jit(solution)/shard_map/jit(cholesky)/cholesky | solution.py:99
  453.9 1.5 convolution_subtract_fusion.5
  455.4 11.7 %cholesky.398 = f32[128,128]{1,0:T(8,128)S(1)} custom-call(f32[128,128]{1,0:T(8,128)S(1)} %cholesky.448), custom_call_target="Cholesky" | custom-call | tf_op jit(solution)/shard_map/jit(cholesky)/cholesky | solution.py:99
  467.3 9.8 %custom-call.36 = f32[1,128,128]{1,2,0:T(8,128)S(1)} custom-call(f32[1,128,128]{2,1,0:T(8,128)S(1)} %get-tuple-element.113), custom_call_target="InvertDiagBlocksLowerTriangular" | custom-call | tf_op jit(solution)/shard_map/jit(cholesky)/cholesky | solution.py:99
  477.4 1.3 convolution_subtract_fusion.9
  478.8 12.0 %cholesky.415 = f32[128,128]{1,0:T(8,128)S(1)} custom-call(f32[128,128]{1,0:T(8,128)S(1)} %convolution_subtract_fusion.9), custom_call_target="Cholesky" | custom-call | tf_op jit(solution)/shard_map/jit(cholesky)/cholesky | solution.py:99
  490.9 0.6 compare_reduce_fusion.8
  491.5 0.7 compare_reduce_fusion.7
  492.2 0.6 compare_reduce_fusion.6
  492.8 0.7 compare_reduce_fusion.5
  496.0 1.2 fusion.4
  497.3 8.6 %while.3 = (s32[]{:T(128)}, f32[512,512]{0,1:T(8,128)S(1)}, s32[4,2]{0,1:T(2,128)S(1)}, f32[4,128,128]{2,1,0:T(8,128)S(1)}, s32[]{:T(128)}) while((s32[]{:T(128)}, f32[512,512]{0,1:T(8,128)S(1)}, s32[4,2]{0,1:T(2,128)S(1)}, f32[4,128,128]{2,1,0:T(8,128)S(1)}, s32[]{:T(128)}) %tuple.83), condition=%wide.while_cond.1, body=%wide.while_body.1.sunk | while | flops 2 | bytes 393329 | solution.py:100
  497.4 0.6 fusion.125
  498.0 1.3 dynamic-slice.15
  500.1 1.3 dynamic-slice.15
  502.3 1.3 dynamic-slice.15
  504.4 1.3 dynamic-slice.15
  505.9 39.3 %custom-call.27 = f32[4,128,128]{1,2,0:T(8,128)S(1)} custom-call(f32[4,128,128]{2,1,0:T(8,128)S(1)} %get-tuple-element.19), custom_call_target="InvertDiagBlocksLowerTriangular" | custom-call | tf_op jit(solution)/shard_map/triangular_solve | solution.py:100
  547.4 0.7 convolution_subtract_fusion.2
  548.5 1.0 constant_dynamic-slice_fusion.2
  549.6 1.3 copy.159
  (147 shorter events, 20.8 us)
Async XLA Ops:
  7.2 51.3 %all-gather.6.cloned.1.call-start = ((), (), s32[]{:S(2)}) async-start(), calls=%async_computation.2 | async-start | bytes 1114112 | tf_op jit(solution)/shard_map/all_gather | solution.py:53
  8.8 240.3 %all-gather.4.cloned.1.call-start = ((), (), s32[]{:S(2)}) async-start(), calls=%async_computation | async-start | bytes 4456448 | tf_op jit(solution)/shard_map/all_gather | solution.py:59
  58.5 2.4 copy-start.1
  147.2 47.8 %copy-start.4 = (f32[1,128,512]{2,1,0:T(8,128)S(1)}, f32[1,128,512]{2,1,0:T(8,128)}, u32[]{:S(2)}) copy-start(f32[1,128,512]{2,1,0:T(8,128)} %param.8) | copy-start | bytes 786436
  198.1 1.8 copy-start.5
  198.1 2.0 copy-start.6
  198.1 2.0 copy-start.7
  198.1 206.3 %all-reduce.4.cloned.1.call-start = ((), (), s32[]{:S(2)}) async-start(), calls=%async_computation.1 | async-start | bytes 2097152 | tf_op jit(solution)/shard_map/psum | solution.py:98
  254.3 20.6 %collective-permute-start = (f32[4,128,128]{2,0,1:T(4,128)S(1)}, f32[4,128,128]{2,0,1:T(4,128)S(1)}, u32[]{:S(2)}, u32[]{:S(2)}) collective-permute-start(f32[4,128,128]{2,0,1:T(4,128)S(1)} %fusion.73), channel_id=1, source_target_pairs={{0,16},{16,0},{32,48},{48,32},{64,80},{80,64},{96,112},{112,96},{1... | collective-permute-start | bytes 786440 | tf_op jit(solution)/shard_map/ppermute | solution.py:10
  257.3 27.1 %collective-permute-start.1 = (f32[4,128,128]{2,0,1:T(4,128)S(1)}, f32[4,128,128]{2,0,1:T(4,128)S(1)}, u32[]{:S(2)}, u32[]{:S(2)}) collective-permute-start(f32[4,128,128]{2,0,1:T(4,128)S(1)} %fusion.76), channel_id=1, source_target_pairs={{0,32},{16,48},{32,0},{48,16},{64,96},{80,112},{96,64},{112,80},{1... | collective-permute-start | bytes 786440 | tf_op jit(solution)/shard_map/ppermute | solution.py:10
  261.9 22.6 %collective-permute-start.2 = (f32[4,128,128]{2,0,1:T(4,128)S(1)}, f32[4,128,128]{2,0,1:T(4,128)S(1)}, u32[]{:S(2)}, u32[]{:S(2)}) collective-permute-start(f32[4,128,128]{2,0,1:T(4,128)S(1)} %fusion.79), channel_id=1, source_target_pairs={{0,64},{16,80},{32,96},{48,112},{64,0},{80,16},{96,32},{112,48},{1... | collective-permute-start | bytes 786440 | tf_op jit(solution)/shard_map/ppermute | solution.py:10
  266.7 17.7 %collective-permute-start.3 = (f32[4,128,128]{2,0,1:T(4,128)S(1)}, f32[4,128,128]{2,0,1:T(4,128)S(1)}, u32[]{:S(2)}, u32[]{:S(2)}) collective-permute-start(f32[4,128,128]{2,0,1:T(4,128)S(1)} %fusion.82), channel_id=1, source_target_pairs={{0,128},{16,144},{32,160},{48,176},{64,192},{80,208},{96,224},{112... | collective-permute-start | bytes 786440 | tf_op jit(solution)/shard_map/ppermute | solution.py:10
  270.3 14.2 %collective-permute-start.4 = (f32[4,128,128]{2,0,1:T(4,128)S(1)}, f32[4,128,128]{2,0,1:T(4,128)S(1)}, u32[]{:S(2)}, u32[]{:S(2)}) collective-permute-start(f32[4,128,128]{2,0,1:T(4,128)S(1)} %fusion.85), channel_id=1, source_target_pairs={{0,256},{16,272},{32,288},{48,304},{64,320},{80,336},{96,352},{112... | collective-permute-start | bytes 786440 | tf_op jit(solution)/shard_map/ppermute | solution.py:10
  286.7 1.0 copy-start.2
  404.4 1.7 copy-start
  406.3 1.0 copy-start.3
Sparse Core Ops, SparseCore 0:
  10.7 47.7 all-gather.5
  198.2 50.7 all-gather.3
  287.9 116.4 all-reduce.3
where the time goes:
time: 567 us; the launch traced here: 558 us
  other arithmetic  242 us (43%)
  waiting for transfers between devices  221 us (39%)
  local copies, waits for them, and re-layouts  33.7 us (6%)
  matrix products  21.9 us (4%)
  between operations  20.2 us (4%)
  starting transfers between devices  18.7 us (3%)
    psum x1, waiting for transfers between devices, per_device(): anc_pivot = lax.psum(contribution, 'front')  114 us
    another operation x15, other arithmetic, per_device(): anc_lower = jnp.linalg.cholesky(anc_pivot)  79.5 us
    another operation x14, other arithmetic, per_device(): lower = jnp.linalg.cholesky(pivot)  79 us
    all_gather x1, waiting for transfers between devices, per_device(): pivot = lax.all_gather(child_pivot[0], 'front', axis=0, tiled=True)  49.6 us
    all_gather x1, waiting for transfers between devices, per_device(): lax.all_gather(panel, 'front', axis=0, tiled=True)  47.6 us
    another operation x4, other arithmetic, per_device(): lax.linalg.triangular_solve(lower, child_panel[0], left_side=False, lower...  41.3 us
    another operation x2, other arithmetic, per_device(): lax.linalg.triangular_solve(anc_lower, assembled, left_side=False, lower=...  40.5 us
    ppermute x5, starting transfers between devices, swapped(): return lax.ppermute(value, axis, pairs)  18.6 us
  transfers between devices with their start and end apart: 8, of which 4 were waited for; matrix products, arithmetic and copies ran while one was open for 1% of the time, Pallas kernels for 0%

commit v1 on v0

--- a/solution.py
+++ b/solution.py
@@ -95,7 +95,7 @@
     contribution = lax.dynamic_update_slice_in_dim(
         jnp.zeros((width, width), jnp.float32), top_rows, owner_pos * block, 0
     )
-    anc_pivot = lax.psum(contribution, "front")
+    anc_pivot = jnp.sum(lax.all_gather(contribution, "front"), axis=0)
     anc_lower = jnp.linalg.cholesky(anc_pivot)
     solved = lax.linalg.triangular_solve(
         anc_lower, assembled, left_side=False, lower=True, transpose_a=True

time: 567 us -> 549 us (0.968)
  waiting for transfers between devices: 221 us -> 204 us
  other arithmetic: 242 us -> 250 us
  local copies, waits for them, and re-layouts: 33.7 us -> 27.5 us
    psum x1 -> x0, waiting for transfers between devices: 114 us -> none  [per_device(): anc_pivot = lax.psum(contribution, 'front')]
    all_gather x0 -> x1, waiting for transfers between devices: none -> 96 us  [per_device(): anc_pivot = jnp.sum(lax.all_gather(contribution, 'front'), axis=0)]
    reduce_sum x0 -> x1, other arithmetic: none -> 7.91 us  [per_device(): anc_pivot = jnp.sum(lax.all_gather(contribution, 'front'), axis=0)]
    another operation x40 -> x27, local copies, waits for them, and re-layouts: 16.8 us -> 16.4 us
where the time goes in v1:
time: 549 us; the launch traced here: 540 us
  other arithmetic  250 us (46%)
  waiting for transfers between devices  204 us (37%)
  local copies, waits for them, and re-layouts  27.5 us (5%)
  between operations  20.1 us (4%)
  matrix products  19.1 us (3%)
  starting transfers between devices  18.7 us (3%)
    all_gather x1, waiting for transfers between devices, per_device(): anc_pivot = jnp.sum(lax.all_gather(contribution, 'front'), axis=0)  96 us
    another operation x15, other arithmetic, per_device(): anc_lower = jnp.linalg.cholesky(anc_pivot)  79.3 us
    another operation x14, other arithmetic, per_device(): lower = jnp.linalg.cholesky(pivot)  78.6 us
    all_gather x1, waiting for transfers between devices, per_device(): pivot = lax.all_gather(child_pivot[0], 'front', axis=0, tiled=True)  49.6 us
    all_gather x1, waiting for transfers between devices, per_device(): lax.all_gather(panel, 'front', axis=0, tiled=True)  49.2 us
    another operation x4, other arithmetic, per_device(): lax.linalg.triangular_solve(lower, child_panel[0], left_side=False, lower...  40.7 us
    another operation x2, other arithmetic, per_device(): lax.linalg.triangular_solve(anc_lower, assembled, left_side=False, lower=...  40.6 us
    ppermute x5, starting transfers between devices, swapped(): return lax.ppermute(value, axis, pairs)  18.6 us
  transfers between devices with their start and end apart: 8, of which 4 were waited for; matrix products, arithmetic and copies ran while one was open for 1% of the time, Pallas kernels for 0%

profile of v1, /device:TPU:1, one launch (start us, length us, event | category | flops | bytes accessed | tf_op | source)
XLA Modules:
  0.0 540.0 jit_solution(6522058480766709280)
XLA Ops:
  7.2 1.5 copy.65
  8.8 49.6 %all-gather.9.cloned.1.call-done = f32[1,512,512]{2,0,1:T(1,128)} async-done(((f32[1,32,512]{2,0,1:T(1,128)}), f32[1,512,512]{2,0,1:T(1,128)}) %all-gather.9.cloned.1.call-update) | async-done | bytes 1048592 | tf_op jit(solution)/shard_map/all_gather | solution.py:53
  58.5 2.4 copy.66
  61.2 11.7 %cholesky.286 = f32[128,128]{1,0:T(8,128)S(1)} custom-call(f32[128,128]{1,0:T(8,128)S(1)} %cholesky.426), custom_call_target="Cholesky" | custom-call | tf_op jit(solution)/shard_map/jit(cholesky)/cholesky | solution.py:54
  73.0 9.8 %custom-call.31 = f32[1,128,128]{1,2,0:T(8,128)S(1)} custom-call(f32[1,128,128]{2,1,0:T(8,128)S(1)} %get-tuple-element.91), custom_call_target="InvertDiagBlocksLowerTriangular" | custom-call | tf_op jit(solution)/shard_map/jit(cholesky)/cholesky | solution.py:54
  83.5 11.7 %cholesky.305 = f32[128,128]{1,0:T(8,128)S(1)} custom-call(f32[128,128]{1,0:T(8,128)S(1)} %cholesky.430), custom_call_target="Cholesky" | custom-call | tf_op jit(solution)/shard_map/jit(cholesky)/cholesky | solution.py:54
  95.3 10.0 %custom-call.32 = f32[1,128,128]{1,2,0:T(8,128)S(1)} custom-call(f32[1,128,128]{2,1,0:T(8,128)S(1)} %get-tuple-element.88), custom_call_target="InvertDiagBlocksLowerTriangular" | custom-call | tf_op jit(solution)/shard_map/jit(cholesky)/cholesky | solution.py:54
  105.9 11.7 %cholesky.326 = f32[128,128]{1,0:T(8,128)S(1)} custom-call(f32[128,128]{1,0:T(8,128)S(1)} %cholesky.435), custom_call_target="Cholesky" | custom-call | tf_op jit(solution)/shard_map/jit(cholesky)/cholesky | solution.py:54
  117.7 9.8 %custom-call.33 = f32[1,128,128]{1,2,0:T(8,128)S(1)} custom-call(f32[1,128,128]{2,1,0:T(8,128)S(1)} %get-tuple-element.85), custom_call_target="InvertDiagBlocksLowerTriangular" | custom-call | tf_op jit(solution)/shard_map/jit(cholesky)/cholesky | solution.py:54
  128.1 11.7 %cholesky.343 = f32[128,128]{1,0:T(8,128)S(1)} custom-call(f32[128,128]{1,0:T(8,128)S(1)} %convolution_subtract_fusion.11), custom_call_target="Cholesky" | custom-call | tf_op jit(solution)/shard_map/jit(cholesky)/cholesky | solution.py:54
  139.9 0.6 compare_reduce_fusion.10
  140.5 0.7 compare_reduce_fusion.9
  141.2 0.6 compare_reduce_fusion.11
  144.8 8.0 %while.2 = (s32[]{:T(128)}, f32[512,512]{1,0:T(8,128)S(1)}, s32[4,2]{0,1:T(2,128)S(1)}, f32[4,128,128]{2,1,0:T(8,128)S(1)}, s32[]{:T(128)}) while((s32[]{:T(128)}, f32[512,512]{1,0:T(8,128)S(1)}, s32[4,2]{0,1:T(2,128)S(1)}, f32[4,128,128]{2,1,0:T(8,128)S(1)}, s32[]{:T(128)}) %tuple.69), condition=%wide.while_cond, body=%wide.while_body.sunk | while | flops 2 | bytes 131189 | solution.py:56
  145.4 1.4 bitcast_dynamic-update-slice_fusion.9
  147.4 1.4 bitcast_dynamic-update-slice_fusion.9
  149.4 1.4 bitcast_dynamic-update-slice_fusion.9
  151.4 1.4 bitcast_dynamic-update-slice_fusion.9
  152.8 39.7 %custom-call.26 = f32[4,128,128]{1,2,0:T(8,128)S(1)} custom-call(f32[4,128,128]{2,1,0:T(8,128)S(1)} %get-tuple-element.11), custom_call_target="InvertDiagBlocksLowerTriangular" | custom-call | tf_op jit(solution)/shard_map/triangular_solve | solution.py:56
  195.0 0.7 pad_maximum_fusion
  197.5 49.2 %all-gather.5.cloned.1.call-done = f32[2048,512]{0,1:T(8,128)} async-done(((f32[128,512]{0,1:T(8,128)}), f32[2048,512]{0,1:T(8,128)}) %all-gather.5.cloned.1.call-update) | async-done | bytes 4194320 | tf_op jit(solution)/shard_map/all_gather | solution.py:59
  246.7 4.5 convolution_bitcast_fusion
  251.9 2.6 collective-permute-start
  254.9 4.0 collective-permute-start.1
  259.5 4.4 collective-permute-start.2
  264.4 3.1 collective-permute-start.3
  268.0 4.5 collective-permute-start.4
  272.5 9.5 %collective-permute-done.1 = f32[4,128,128]{2,0,1:T(4,128)S(1)} collective-permute-done((f32[4,128,128]{2,0,1:T(4,128)S(1)}, f32[4,128,128]{2,0,1:T(4,128)S(1)}, u32[]{:S(2)}, u32[]{:S(2)}) %collective-permute-start.1) | collective-permute-done | bytes 262176 | tf_op jit(solution)/shard_map/ppermute | solution.py:10
  282.2 1.2 convolution_bitcast_fusion.1
  283.6 1.0 copy-done.4
  285.0 1.0 copy-done.1
  286.0 0.8 copy.75
  286.9 0.6 dynamic-slice_bitcast_fusion
  287.5 96.0 %all-gather.7.cloned.1.call-done = f32[16,512,512]{2,1,0:T(8,128)} async-done(((f32[1,512,512]{2,1,0:T(8,128)}), f32[16,512,512]{2,1,0:T(8,128)}) %all-gather.7.cloned.1.call-update) | async-done | bytes 16777232 | tf_op jit(solution)/shard_map/all_gather | solution.py:98
  383.5 7.9 %reduce_sum.79 = f32[512,512]{1,0:T(8,128)S(1)} reduce(f32[16,512,512]{2,1,0:T(8,128)} %all-gather.7.cloned.1.call-done, f32[]{:T(128)} %constant.143.clone.1), dimensions={0}, to_apply=%region_15.17 | reduce | flops 3932160 | bytes 17825796 | tf_op jit(solution)/shard_map/reduce_sum | solution.py:98
  392.0 1.0 copy-done.2
  392.9 11.7 %cholesky.358 = f32[128,128]{1,0:T(8,128)S(1)} custom-call(f32[128,128]{1,0:T(8,128)S(1)} %cholesky.439), custom_call_target="Cholesky" | custom-call | tf_op jit(solution)/shard_map/jit(cholesky)/cholesky | solution.py:99
  404.8 9.8 %custom-call.34 = f32[1,128,128]{1,2,0:T(8,128)S(1)} custom-call(f32[1,128,128]{2,1,0:T(8,128)S(1)} %get-tuple-element.81), custom_call_target="InvertDiagBlocksLowerTriangular" | custom-call | tf_op jit(solution)/shard_map/jit(cholesky)/cholesky | solution.py:99
  415.3 11.9 %cholesky.377 = f32[128,128]{1,0:T(8,128)S(1)} custom-call(f32[128,128]{1,0:T(8,128)S(1)} %cholesky.443), custom_call_target="Cholesky" | custom-call | tf_op jit(solution)/shard_map/jit(cholesky)/cholesky | solution.py:99
  427.3 9.8 %custom-call.35 = f32[1,128,128]{1,2,0:T(8,128)S(1)} custom-call(f32[1,128,128]{2,1,0:T(8,128)S(1)} %get-tuple-element.78), custom_call_target="InvertDiagBlocksLowerTriangular" | custom-call | tf_op jit(solution)/shard_map/jit(cholesky)/cholesky | solution.py:99
  437.8 11.7 %cholesky.398 = f32[128,128]{1,0:T(8,128)S(1)} custom-call(f32[128,128]{1,0:T(8,128)S(1)} %cholesky.448), custom_call_target="Cholesky" | custom-call | tf_op jit(solution)/shard_map/jit(cholesky)/cholesky | solution.py:99
  449.5 9.8 %custom-call.36 = f32[1,128,128]{1,2,0:T(8,128)S(1)} custom-call(f32[1,128,128]{2,1,0:T(8,128)S(1)} %get-tuple-element.75), custom_call_target="InvertDiagBlocksLowerTriangular" | custom-call | tf_op jit(solution)/shard_map/jit(cholesky)/cholesky | solution.py:99
  459.5 0.6 convolution_subtract_fusion.9
  460.2 11.7 %cholesky.415 = f32[128,128]{1,0:T(8,128)S(1)} custom-call(f32[128,128]{1,0:T(8,128)S(1)} %convolution_subtract_fusion.9), custom_call_target="Cholesky" | custom-call | tf_op jit(solution)/shard_map/jit(cholesky)/cholesky | solution.py:99
  471.9 0.6 compare_reduce_fusion.8
  472.6 0.7 compare_reduce_fusion.7
  473.3 0.6 compare_reduce_fusion.6
  473.9 0.7 compare_reduce_fusion.5
  477.1 1.2 fusion.4
  478.4 8.1 %while.3 = (s32[]{:T(128)}, f32[512,512]{1,0:T(8,128)S(1)}, s32[4,2]{0,1:T(2,128)S(1)}, f32[4,128,128]{2,1,0:T(8,128)S(1)}, s32[]{:T(128)}) while((s32[]{:T(128)}, f32[512,512]{1,0:T(8,128)S(1)}, s32[4,2]{0,1:T(2,128)S(1)}, f32[4,128,128]{2,1,0:T(8,128)S(1)}, s32[]{:T(128)}) %tuple.81), condition=%wide.while_cond.1, body=%wide.while_body.1.sunk | while | flops 2 | bytes 131189 | solution.py:100
  478.4 0.6 fusion.126
  479.0 1.3 bitcast_dynamic-update-slice_fusion.10
  480.5 0.6 fusion.126
  481.1 1.3 bitcast_dynamic-update-slice_fusion.10
  482.5 0.6 fusion.126
  483.1 1.3 bitcast_dynamic-update-slice_fusion.10
  484.6 0.6 fusion.126
  485.2 1.3 bitcast_dynamic-update-slice_fusion.10
  486.5 39.3 %custom-call.27 = f32[4,128,128]{1,2,0:T(8,128)S(1)} custom-call(f32[4,128,128]{2,1,0:T(8,128)S(1)} %get-tuple-element.19), custom_call_target="InvertDiagBlocksLowerTriangular" | custom-call | tf_op jit(solution)/shard_map/triangular_solve | solution.py:100
  526.3 0.6 convolution_subtract_fusion.1
  527.3 1.0 convolution_subtract_fusion
  528.7 1.5 convolution_subtract_fusion.2
  530.9 1.0 constant_dynamic-slice_fusion.2
  531.9 1.1 fusion.1
  (116 shorter events, 17.2 us)
Async XLA Ops:
  7.2 51.3 %all-gather.9.cloned.1.call-start = ((), (), s32[]{:S(2)}) async-start(), calls=%async_computation.2 | async-start | bytes 1114112 | tf_op jit(solution)/shard_map/all_gather | solution.py:53
  8.8 237.9 %all-gather.5.cloned.1.call-start = ((), (), s32[]{:S(2)}) async-start(), calls=%async_computation | async-start | bytes 4456448 | tf_op jit(solution)/shard_map/all_gather | solution.py:59
  58.5 2.4 copy-start
  144.5 48.1 %copy-start.5 = (f32[1,128,512]{2,1,0:T(8,128)S(1)}, f32[1,128,512]{2,1,0:T(8,128)}, u32[]{:S(2)}) copy-start(f32[1,128,512]{2,1,0:T(8,128)} %param.8) | copy-start | bytes 786436
  193.1 2.7 copy-start.6
  193.2 2.9 copy-start.7
  193.2 2.9 copy-start.8
  195.7 187.7 %all-gather.7.cloned.1.call-start = ((), (), s32[]{:S(2)}) async-start(), calls=%async_computation.1 | async-start | bytes 17825792 | tf_op jit(solution)/shard_map/all_gather | solution.py:98
  251.9 20.6 %collective-permute-start = (f32[4,128,128]{2,0,1:T(4,128)S(1)}, f32[4,128,128]{2,0,1:T(4,128)S(1)}, u32[]{:S(2)}, u32[]{:S(2)}) collective-permute-start(f32[4,128,128]{2,0,1:T(4,128)S(1)} %fusion.74), channel_id=1, source_target_pairs={{0,16},{16,0},{32,48},{48,32},{64,80},{80,64},{96,112},{112,96},{1... | collective-permute-start | bytes 786440 | tf_op jit(solution)/shard_map/ppermute | solution.py:10
  254.9 27.1 %collective-permute-start.1 = (f32[4,128,128]{2,0,1:T(4,128)S(1)}, f32[4,128,128]{2,0,1:T(4,128)S(1)}, u32[]{:S(2)}, u32[]{:S(2)}) collective-permute-start(f32[4,128,128]{2,0,1:T(4,128)S(1)} %fusion.77), channel_id=1, source_target_pairs={{0,32},{16,48},{32,0},{48,16},{64,96},{80,112},{96,64},{112,80},{1... | collective-permute-start | bytes 786440 | tf_op jit(solution)/shard_map/ppermute | solution.py:10
  259.5 22.6 %collective-permute-start.2 = (f32[4,128,128]{2,0,1:T(4,128)S(1)}, f32[4,128,128]{2,0,1:T(4,128)S(1)}, u32[]{:S(2)}, u32[]{:S(2)}) collective-permute-start(f32[4,128,128]{2,0,1:T(4,128)S(1)} %fusion.80), channel_id=1, source_target_pairs={{0,64},{16,80},{32,96},{48,112},{64,0},{80,16},{96,32},{112,48},{1... | collective-permute-start | bytes 786440 | tf_op jit(solution)/shard_map/ppermute | solution.py:10
  264.4 17.7 %collective-permute-start.3 = (f32[4,128,128]{2,0,1:T(4,128)S(1)}, f32[4,128,128]{2,0,1:T(4,128)S(1)}, u32[]{:S(2)}, u32[]{:S(2)}) collective-permute-start(f32[4,128,128]{2,0,1:T(4,128)S(1)} %fusion.83), channel_id=1, source_target_pairs={{0,128},{16,144},{32,160},{48,176},{64,192},{80,208},{96,224},{112... | collective-permute-start | bytes 786440 | tf_op jit(solution)/shard_map/ppermute | solution.py:10
  268.0 14.2 %collective-permute-start.4 = (f32[4,128,128]{2,0,1:T(4,128)S(1)}, f32[4,128,128]{2,0,1:T(4,128)S(1)}, u32[]{:S(2)}, u32[]{:S(2)}) collective-permute-start(f32[4,128,128]{2,0,1:T(4,128)S(1)} %fusion.86), channel_id=1, source_target_pairs={{0,256},{16,272},{32,288},{48,304},{64,320},{80,336},{96,352},{112... | collective-permute-start | bytes 786440 | tf_op jit(solution)/shard_map/ppermute | solution.py:10
  283.4 1.2 copy-start.4
  285.0 1.0 copy-start.1
  392.0 1.0 copy-start.2
  392.9 21.7 %copy-start.3 = (f32[512,512]{1,0:T(8,128)S(1)}, f32[512,512]{1,0:T(8,128)}, u32[]{:S(2)}) copy-start(f32[512,512]{1,0:T(8,128)} %copy-done.2) | copy-start | bytes 3145732
Sparse Core Ops, SparseCore 0:
  10.7 47.7 all-gather.8
  195.8 50.8 all-gather.4
  286.1 97.2 all-gather.6
